TPU v7x, 32 devices: a whole 2x2x4 slice. The times are simulated.
32 devices in a mesh: col: 8 (over z, y), row: 4 (over x, core).
Axes of the slice: x: 2, y: 2, z: 4, core: 2. Of those that a mesh axis runs over, the one named last changes fastest.
Arguments:
- factor: float32 [8, 512, 1024], P('col', 'row'), may hold values from -0.6 to 0.6
- pattern: int32 [8, 4, 8], replicated, may hold values from 0 to 1, as said below
- order: int32 [8], replicated, may hold values from 0 to 7, each once
- targets: int32 [2, 2], replicated, may hold values from 0 to 3, as said below
- panels: float32 [512, 512], P('row'), may hold values from -6 to 6
Outputs:
- carried: float32 [8, 512, 512], P('col', 'row')
Inputs may be any that keep to these rules, and one draw needn't show every extreme that they name: `pattern`: 0 or 1 for each block of a supernode's rows and factored columns; the share of present blocks differs between supernodes. `targets`: every row block 0..3 is named at least once.
All inputs are finite; a program needn't handle non-finite values.
Results may differ from a plain program's by a relative error of at most 0.0001.
Values sent between devices are 32-bit elements; how exact they have to be, the bound alone decides.
No kernel may reach another device: no remote copies, remote signals or barrier semaphores. Data moves between devices by JAX's collectives and lax.ppermute only.
A program may use at most 128 MiB of HBM per device.

v0:
```python
import functools

import jax
import jax.numpy as jnp
from jax import lax
from jax.experimental import pallas as pl
from jax.experimental.pallas import tpu as pltpu
from jax.sharding import PartitionSpec as P


BLOCK = 128
HALF = BLOCK // 2
PARAMS = pltpu.CompilerParams(vmem_limit_bytes=8 << 20)
NT = (((1,), (1,)), ((), ()))
SMEM = pl.BlockSpec(memory_space=pltpu.SMEM)
VMEM = pl.BlockSpec(memory_space=pltpu.VMEM)
ANY = pl.BlockSpec(memory_space=pl.ANY)
HBM = pl.BlockSpec(memory_space=pltpu.HBM)
F32, BF16 = jnp.float32, jnp.bfloat16


def odd(place, bits):
    parity = place & 1
    for k in range(1, bits):
        parity ^= (place >> k) & 1
    return parity


def halves(value):
    high = value.astype(BF16)
    return high, (value - high.astype(F32)).astype(BF16)


def product(left, right):
    dot = functools.partial(lax.dot_general, dimension_numbers=NT, preferred_element_type=F32)
    return dot(left[0], right[0]) + (dot(left[0], right[1]) + dot(left[1], right[0]))


def masked(ref, present_ref, row):
    parts = []
    for k in range(ref.shape[1] // BLOCK):
        keep = present_ref[row, k].astype(F32)
        parts.append(ref[:, k * BLOCK : (k + 1) * BLOCK] * keep)
    return jnp.concatenate(parts, axis=1)


def left_lanes(shape):
    return lax.broadcasted_iota(jnp.int32, shape, 1) < HALF


def near_kernel(bits, order_ref, pattern_ref, own_hbm, sibling_ref, out_ref, high_ref, low_ref, present_ref, own_ref, sems):
    row, place = lax.axis_index("row"), lax.axis_index("col")
    rows = pltpu.make_async_copy(own_hbm, own_ref, sems.at[0])
    rows.start()
    cells = pltpu.make_async_copy(pattern_ref.at[order_ref[place]], present_ref, sems.at[1])
    cells.start()
    cells.wait()
    sibling = halves(masked(sibling_ref, present_ref, row ^ 1))
    rows.wait()
    own = halves(masked(own_ref, present_ref, row))
    diagonal = product(own, own)
    out_ref[0:HALF] = diagonal[0:HALF]
    corner, quarter = diagonal[HALF:], HALF // 2
    moved = pltpu.roll(corner[0:quarter], HALF, axis=1)
    out_ref[HALF : HALF + quarter] = jnp.where(left_lanes(moved.shape), moved, corner[quarter:])
    first = (row & 1) == 0
    shared = product(
        [jnp.where(first, a[0:HALF], b[HALF:]) for a, b in zip(own, sibling, strict=True)],
        [jnp.where(first, b, a) for a, b in zip(own, sibling, strict=True)],
    )
    out_ref[HALF + quarter :] = shared
    plain = (((row >> 1) & 1) ^ odd(place, bits)) == 0
    for kept, mine, theirs in zip((high_ref, low_ref), own, sibling, strict=True):
        kept[...] = jnp.where(plain, mine, theirs)


def far_kernel(bits, present_ref, high_ref, low_ref, across_ref, out_ref):
    row = lax.axis_index("row") ^ odd(lax.axis_index("col"), bits)
    across = halves(masked(across_ref, present_ref, row ^ 2))
    out_ref[...] = product(across, (high_ref[...], low_ref[...]))


def columns_of(j, targets_ref, slot):
    return (targets_ref[slot // targets_ref.shape[1], slot % targets_ref.shape[1]] ^ lax.axis_index("row")) == j


def write(values, targets_ref, panels_ref, out_hbm, staged_ref, sems):
    slots = range(targets_ref.shape[0] * targets_ref.shape[1])
    for wait in (False, True):
        for j, value in values.items():
            for slot in slots:
                columns = slice(slot * BLOCK, (slot + 1) * BLOCK)
                copy = pltpu.make_async_copy(staged_ref.at[slot], out_hbm.at[:, columns], sems.at[slot])

                @pl.when(columns_of(j, targets_ref, slot))
                def _():
                    if wait:
                        copy.wait()
                    else:
                        staged_ref[slot] = panels_ref[:, columns] - value
                        copy.start()


def near_finish_kernel(targets_ref, panels_ref, near_ref, beside_ref, out_hbm, staged_ref, sems):
    quarter = HALF // 2
    upper = near_ref[0:HALF]
    turned = jnp.concatenate([upper, upper]).T[HALF:]
    corner = near_ref[HALF : HALF + quarter]
    corner = jnp.concatenate([pltpu.roll(corner, HALF, axis=1), corner])
    diagonal = jnp.concatenate([upper, jnp.where(left_lanes(corner.shape), turned, corner)])
    first = (lax.axis_index("row") & 1) == 0
    mine, theirs = near_ref[HALF + quarter :], beside_ref[...]
    shared = jnp.concatenate([jnp.where(first, mine, theirs), jnp.where(first, theirs, mine)])
    shared = jnp.where(first, shared, shared.T)
    write({0: diagonal, 1: shared}, targets_ref, panels_ref, out_hbm, staged_ref, sems)


def far_finish_kernel(bits, targets_ref, panels_ref, own_ref, across_ref, beside_ref, begun_hbm, out_hbm, staged_ref, sems):
    del begun_hbm
    second = (lax.axis_index("row") >> 1) & 1
    plain = (second ^ odd(lax.axis_index("col"), bits)) == 0
    turned = jnp.where(plain, own_ref[...], beside_ref[...]).T
    straight, first = across_ref[...], second == 0
    write(
        {2: jnp.where(first, turned, straight), 3: jnp.where(first, straight, turned)},
        targets_ref,
        panels_ref,
        out_hbm,
        staged_ref,
        sems,
    )


def moved(value, to):
    columns, rows = lax.axis_size("col"), lax.axis_size("row")
    pairs = []
    for place in range(columns):
        for row in range(rows):
            there, other = to(place, row)
            pairs.append((place * rows + row, there * rows + other))
    return lax.ppermute(value, ("col", "row"), pairs)


def scanned(update, turn):
    place, size = lax.axis_index("col"), lax.axis_size("col")
    inclusive, total, bit = update, update, 1
    while bit < size:
        other = moved(total, lambda p, r, bit=bit: (p ^ bit, r ^ turn))
        inclusive = inclusive + jnp.where((place & bit) != 0, other, 0.0)
        total = total + other
        bit = bit * 2
    return inclusive


def kernel(call, **kwargs):
    def run(*args):
        return pl.pallas_call(call, compiler_params=PARAMS, **kwargs)(*args)

    return run


def body(factor, pattern, order, targets, panels):
    own = factor[0]
    rows, width = own.shape
    bits = (lax.axis_size("col") - 1).bit_length()
    cost = functools.partial(pl.CostEstimate, transcendentals=0)
    flops = 2 * 3 * rows * BLOCK * width
    sibling = moved(own, lambda p, r: (p, r ^ 1))
    across = moved(own, lambda p, r: (p, r ^ 2 ^ odd(p, bits)))
    near, high, low, present = kernel(
        functools.partial(near_kernel, bits),
        out_shape=[
            jax.ShapeDtypeStruct((BLOCK + HALF // 2, BLOCK), F32),
            jax.ShapeDtypeStruct((rows, width), BF16),
            jax.ShapeDtypeStruct((rows, width), BF16),
            jax.ShapeDtypeStruct(pattern.shape[1:], jnp.int32),
        ],
        in_specs=[SMEM, HBM, HBM, VMEM],
        out_specs=[VMEM, VMEM, VMEM, SMEM],
        scratch_shapes=[pltpu.VMEM((rows, width), F32), pltpu.SemaphoreType.DMA((2,))],
        cost_estimate=cost(flops=2 * flops, bytes_accessed=12 * rows * width),
    )(order, pattern, own, sibling)
    near_sum = scanned(near, 0)
    far = kernel(
        functools.partial(far_kernel, bits),
        out_shape=jax.ShapeDtypeStruct((rows, rows), F32),
        in_specs=[SMEM, VMEM, VMEM, VMEM],
        out_specs=VMEM,
        cost_estimate=cost(flops=flops, bytes_accessed=8 * rows * width),
    )(present, high, low, across)
    far_sum = scanned(far, 1)
    shared = moved(near_sum[HALF + HALF // 2 :], lambda p, r: (p, r ^ 1))
    theirs = moved(far_sum, lambda p, r: (p, r ^ 2 ^ odd(p, bits)))
    beside = moved(far_sum, lambda p, r: (p, r ^ 1))
    slots = targets.shape[0] * targets.shape[1]
    writing = dict(
        out_shape=jax.ShapeDtypeStruct(panels.shape, F32),
        out_specs=ANY,
        scratch_shapes=[pltpu.VMEM((slots, rows, BLOCK), F32), pltpu.SemaphoreType.DMA((slots,))],
        cost_estimate=cost(flops=0, bytes_accessed=12 * rows * panels.shape[1]),
    )
    begun = kernel(near_finish_kernel, in_specs=[SMEM] + [VMEM] * 3, **writing)(targets, panels, near_sum, shared)
    carried = kernel(
        functools.partial(far_finish_kernel, bits),
        in_specs=[SMEM] + [VMEM] * 4 + [ANY],
        input_output_aliases={5: 0},
        **writing,
    )(targets, panels, far_sum, theirs, beside, begun)
    return carried[None]


def solution(mesh):
    placed = (P("col", "row", None), P(), P(), P(), P("row", None))
    return jax.shard_map(
        body, mesh=mesh, in_specs=placed, out_specs=P("col", "row", None), check_vma=False
    )
```

profile of v0, /device:TPU:0, one launch (start us, length us, event | category | flops | bytes accessed | tf_op | source)
XLA Modules:
  0.0 39.7 jit_solution(1644328490488966271)
XLA Ops:
  0.0 0.0 copy-start.4
  0.0 0.5 %collective-permute-start = (f32[128,1024]{1,0:T(8,128)}, f32[128,1024]{1,0:T(8,128)S(1)}, u32[]{:S(2)}, u32[]{:S(2)}) collective-permute-start(f32[128,1024]{1,0:T(8,128)} %bitcast.2), channel_id=1, source_target_pairs={{0,1},{1,0},{2,3},{3,2},{4,5},{5,4},{6,7},{7,6},{8,9},{9,8},{10,11... | collective-permute-start | bytes 1572872 | tf_op jit(solution)/shard_map/ppermute | solution.py:141
  0.5 2.5 %collective-permute-start.1 = (f32[128,1024]{1,0:T(8,128)}, f32[128,1024]{1,0:T(8,128)S(1)}, u32[]{:S(2)}, u32[]{:S(2)}) collective-permute-start(f32[128,1024]{1,0:T(8,128)} %bitcast.3), channel_id=1, source_target_pairs={{0,2},{1,3},{2,0},{3,1},{4,7},{5,6},{6,5},{7,4},{8,11},{9,10},{10,... | collective-permute-start | bytes 1572872 | tf_op jit(solution)/shard_map/ppermute | solution.py:141
  3.0 0.0 collective-permute-done.sibling_ref
  3.0 0.0 copy-done.4
  3.0 0.0 copy-start.1
  3.0 1.1 %copy-done.1 = f32[1,128,1024]{2,1,0:T(8,128)S(1)} copy-done((f32[1,128,1024]{2,1,0:T(8,128)S(1)}, f32[1,128,1024]{2,1,0:T(8,128)}, u32[]{:S(2)}) %copy-start.1) | copy-done | bytes 524312
  4.1 0.0 copy-start.2
  4.1 0.7 %copy-done.2 = s32[8,4,8]{2,1,0:T(4,128)S(1)} copy-done((s32[8,4,8]{2,1,0:T(4,128)S(1)}, s32[8,4,8]{2,1,0:T(4,128)}, u32[]{:S(2)}) %copy-start.2) | copy-done | bytes 1048
  4.8 2.0 %shard_map.55 = (f32[160,128]{1,0:T(8,128)S(1)}, bf16[128,1024]{1,0:T(8,128)(2,1)S(1)}, bf16[128,1024]{1,0:T(8,128)(2,1)S(1)}, s32[4,8]{1,0:T(4,128)S(1)}) custom-call(s32[8]{0:T(128)S(1)} %copy-done.4, s32[8,4,8]{2,1,0:T(4,128)S(1)} %copy-done.2, f32[128,1024]{1,0:T(8,128)S(1)} %bitcast.4, f32[128,1024]{1,0:T(8,128)S(1)} %collective-permute-done.sibling_ref), custom_call_target="tpu_custom_call" | custom-call | flops 201326592 | bytes 1572864 | tf_op jit(solution)/shard_map/pallas_call | solution.py:157
  6.8 9.0 %collective-permute-done.1.across_ref = f32[128,1024]{1,0:T(8,128)S(1)} collective-permute-done((f32[128,1024]{1,0:T(8,128)}, f32[128,1024]{1,0:T(8,128)S(1)}, u32[]{:S(2)}, u32[]{:S(2)}) %collective-permute-start.1) | collective-permute-done | bytes 524320 | tf_op jit(solution)/shard_map/ppermute | solution.py:141
  15.8 0.9 %shard_map.56 = f32[128,128]{1,0:T(8,128)S(1)} custom-call(s32[4,8]{1,0:T(4,128)S(1)} %get-tuple-element.9.present_ref, bf16[128,1024]{1,0:T(8,128)(2,1)S(1)} %get-tuple-element.10.high_ref, bf16[128,1024]{1,0:T(8,128)(2,1)S(1)} %get-tuple-element.11.low_ref, f32[128,1024]{1,0:T(8,128)S(1)} %collective-permute-done.1.across_ref), custom_call_target="tpu_custom_call" | custom-call | flops 100663296 | bytes 1048576 | tf_op jit(solution)/shard_map/pallas_call | solution.py:157
  16.7 1.2 %collective-permute-start.2 = (f32[128,128]{1,0:T(8,128)S(1)}, f32[128,128]{1,0:T(8,128)S(1)}, u32[]{:S(2)}, u32[]{:S(2)}) collective-permute-start(f32[128,128]{1,0:T(8,128)S(1)} %shard_map.56), channel_id=1, source_target_pairs={{0,5},{1,4},{2,7},{3,6},{4,1},{5,0},{6,3},{7,2},{8,13},{9,12},{10,... | collective-permute-start | bytes 196616 | tf_op jit(solution)/shard_map/ppermute | solution.py:141
  17.9 0.4 collective-permute-start.7
  18.3 2.8 %collective-permute-done.2 = f32[128,128]{1,0:T(8,128)S(1)} collective-permute-done((f32[128,128]{1,0:T(8,128)S(1)}, f32[128,128]{1,0:T(8,128)S(1)}, u32[]{:S(2)}, u32[]{:S(2)}) %collective-permute-start.2) | collective-permute-done | bytes 65568 | tf_op jit(solution)/shard_map/ppermute | solution.py:141
  21.1 0.8 %collective-permute-start.3 = (f32[128,128]{1,0:T(8,128)S(1)}, f32[128,128]{1,0:T(8,128)S(1)}, u32[]{:S(2)}, u32[]{:S(2)}) collective-permute-start(f32[128,128]{1,0:T(8,128)S(1)} %add.31), channel_id=1, source_target_pairs={{0,9},{1,8},{2,11},{3,10},{4,13},{5,12},{6,15},{7,14},{8,1},{9,0},... | collective-permute-start | bytes 196616 | tf_op jit(solution)/shard_map/ppermute | solution.py:141
  21.9 1.0 %collective-permute-done.7 = f32[160,128]{1,0:T(8,128)S(1)} collective-permute-done((f32[160,128]{1,0:T(8,128)S(1)}, f32[160,128]{1,0:T(8,128)S(1)}, u32[]{:S(2)}, u32[]{:S(2)}) %collective-permute-start.7) | collective-permute-done | bytes 81952 | tf_op jit(solution)/shard_map/ppermute | solution.py:141
  23.0 1.7 %collective-permute-start.8 = (f32[160,128]{1,0:T(8,128)S(1)}, f32[160,128]{1,0:T(8,128)S(1)}, u32[]{:S(2)}, u32[]{:S(2)}) collective-permute-start(f32[160,128]{1,0:T(8,128)S(1)} %add.36), channel_id=1, source_target_pairs={{0,8},{1,9},{2,10},{3,11},{4,12},{5,13},{6,14},{7,15},{8,0},{9,1},... | collective-permute-start | bytes 245768 | tf_op jit(solution)/shard_map/ppermute | solution.py:141
  24.7 0.6 %collective-permute-done.3 = f32[128,128]{1,0:T(8,128)S(1)} collective-permute-done((f32[128,128]{1,0:T(8,128)S(1)}, f32[128,128]{1,0:T(8,128)S(1)}, u32[]{:S(2)}, u32[]{:S(2)}) %collective-permute-start.3) | collective-permute-done | bytes 65568 | tf_op jit(solution)/shard_map/ppermute | solution.py:141
  25.3 1.9 %collective-permute-start.4 = (f32[128,128]{1,0:T(8,128)S(1)}, f32[128,128]{1,0:T(8,128)S(1)}, u32[]{:S(2)}, u32[]{:S(2)}) collective-permute-start(f32[128,128]{1,0:T(8,128)S(1)} %add.33), channel_id=1, source_target_pairs={{0,17},{1,16},{2,19},{3,18},{4,21},{5,20},{6,23},{7,22},{8,25},{9,... | collective-permute-start | bytes 196616 | tf_op jit(solution)/shard_map/ppermute | solution.py:141
  27.2 0.3 collective-permute-done.8
  27.5 2.8 %collective-permute-start.9 = (f32[160,128]{1,0:T(8,128)S(1)}, f32[160,128]{1,0:T(8,128)S(1)}, u32[]{:S(2)}, u32[]{:S(2)}) collective-permute-start(f32[160,128]{1,0:T(8,128)S(1)} %add.38), channel_id=1, source_target_pairs={{0,16},{1,17},{2,18},{3,19},{4,20},{5,21},{6,22},{7,23},{8,24},{9,... | collective-permute-start | bytes 245768 | tf_op jit(solution)/shard_map/ppermute | solution.py:141
  30.2 0.2 collective-permute-done.4
  30.4 0.0 copy-start
  30.4 3.3 %collective-permute-start.5 = (f32[128,128]{1,0:T(8,128)S(1)}, f32[128,128]{1,0:T(8,128)S(1)}, u32[]{:S(2)}, u32[]{:S(2)}) collective-permute-start(f32[128,128]{1,0:T(8,128)S(1)} %select_add_fusion.1.own_ref), channel_id=1, source_target_pairs={{0,2},{1,3},{2,0},{3,1},{4,7},{5,6},{6,5},{7,4},{8,11},{9,10},{10,... | collective-permute-start | bytes 196616 | tf_op jit(solution)/shard_map/ppermute | solution.py:141
  33.7 0.1 collective-permute-start.6
  33.8 1.8 %collective-permute-done.9 = f32[160,128]{1,0:T(8,128)S(1)} collective-permute-done((f32[160,128]{1,0:T(8,128)S(1)}, f32[160,128]{1,0:T(8,128)S(1)}, u32[]{:S(2)}, u32[]{:S(2)}) %collective-permute-start.9) | collective-permute-done | bytes 81952 | tf_op jit(solution)/shard_map/ppermute | solution.py:141
  35.6 0.0 copy-start.3
  35.6 0.1 collective-permute-start.10
  35.7 1.2 %collective-permute-done.10.beside_ref = f32[64,128]{1,0:T(8,128)S(1)} collective-permute-done((f32[64,128]{1,0:T(8,128)S(1)}, f32[64,128]{1,0:T(8,128)S(1)}, u32[]{:S(2)}, u32[]{:S(2)}) %collective-permute-start.10) | collective-permute-done | bytes 32800 | tf_op jit(solution)/shard_map/ppermute | solution.py:141
  36.9 0.0 copy-done
  36.9 0.0 copy-done.3
  36.9 1.4 %shard_map.57.begun_hbm = f32[128,512]{1,0:T(8,128)} custom-call(s32[2,2]{1,0:T(2,128)S(1)} %copy-done.3, f32[128,512]{1,0:T(8,128)S(1)} %copy-done, f32[160,128]{1,0:T(8,128)S(1)} %select_add_fusion.near_ref, f32[64,128]{1,0:T(8,128)S(1)} %collective-permute-done.10.beside_ref), custom_call_target="tpu_custom_call" | custom-call | bytes 786432 | tf_op jit(solution)/shard_map/pallas_call | solution.py:157
  38.3 0.0 collective-permute-done.5.across_ref
  38.3 0.0 collective-permute-done.6.beside_ref
  38.3 1.4 %shard_map.58 = f32[128,512]{1,0:T(8,128)} custom-call(s32[2,2]{1,0:T(2,128)S(1)} %copy-done.3, f32[128,512]{1,0:T(8,128)S(1)} %copy-done, f32[128,128]{1,0:T(8,128)S(1)} %select_add_fusion.1.own_ref, f32[128,128]{1,0:T(8,128)S(1)} %collective-permute-done.5.across_ref, ...), custom_call_target="tpu_custom_call", output_to_operand_aliasing={{}: (5, {})} | custom-call | bytes 786432 | tf_op jit(solution)/shard_map/pallas_call | solution.py:157
  (7 shorter events, 0.1 us)
Async XLA Ops:
  0.0 3.0 %copy-start.4 = (s32[8]{0:T(128)S(1)}, s32[8]{0:T(128)}, u32[]{:S(2)}) copy-start(s32[8]{0:T(128)} %order_ref.1) | copy-start | bytes 100
  0.0 3.0 %collective-permute-start = (f32[128,1024]{1,0:T(8,128)}, f32[128,1024]{1,0:T(8,128)S(1)}, u32[]{:S(2)}, u32[]{:S(2)}) collective-permute-start(f32[128,1024]{1,0:T(8,128)} %bitcast.2), channel_id=1, source_target_pairs={{0,1},{1,0},{2,3},{3,2},{4,5},{5,4},{6,7},{7,6},{8,9},{9,8},{10,11... | collective-permute-start | bytes 1572872 | tf_op jit(solution)/shard_map/ppermute | solution.py:141
  0.5 15.3 %collective-permute-start.1 = (f32[128,1024]{1,0:T(8,128)}, f32[128,1024]{1,0:T(8,128)S(1)}, u32[]{:S(2)}, u32[]{:S(2)}) collective-permute-start(f32[128,1024]{1,0:T(8,128)} %bitcast.3), channel_id=1, source_target_pairs={{0,2},{1,3},{2,0},{3,1},{4,7},{5,6},{6,5},{7,4},{8,11},{9,10},{10,... | collective-permute-start | bytes 1572872 | tf_op jit(solution)/shard_map/ppermute | solution.py:141
  3.0 1.1 %copy-start.1 = (f32[1,128,1024]{2,1,0:T(8,128)S(1)}, f32[1,128,1024]{2,1,0:T(8,128)}, u32[]{:S(2)}) copy-start(f32[1,128,1024]{2,1,0:T(8,128)} %param.5) | copy-start | bytes 1572868
  4.1 0.7 %copy-start.2 = (s32[8,4,8]{2,1,0:T(4,128)S(1)}, s32[8,4,8]{2,1,0:T(4,128)}, u32[]{:S(2)}) copy-start(s32[8,4,8]{2,1,0:T(4,128)} %pattern_ref.1) | copy-start | bytes 3076
  16.7 4.4 %collective-permute-start.2 = (f32[128,128]{1,0:T(8,128)S(1)}, f32[128,128]{1,0:T(8,128)S(1)}, u32[]{:S(2)}, u32[]{:S(2)}) collective-permute-start(f32[128,128]{1,0:T(8,128)S(1)} %shard_map.56), channel_id=1, source_target_pairs={{0,5},{1,4},{2,7},{3,6},{4,1},{5,0},{6,3},{7,2},{8,13},{9,12},{10,... | collective-permute-start | bytes 196616 | tf_op jit(solution)/shard_map/ppermute | solution.py:141
  17.9 5.0 %collective-permute-start.7 = (f32[160,128]{1,0:T(8,128)S(1)}, f32[160,128]{1,0:T(8,128)S(1)}, u32[]{:S(2)}, u32[]{:S(2)}) collective-permute-start(f32[160,128]{1,0:T(8,128)S(1)} %get-tuple-element.12), channel_id=1, source_target_pairs={{0,4},{1,5},{2,6},{3,7},{4,0},{5,1},{6,2},{7,3},{8,12},{9,13},{10,... | collective-permute-start | bytes 245768 | tf_op jit(solution)/shard_map/ppermute | solution.py:141
  21.1 4.2 %collective-permute-start.3 = (f32[128,128]{1,0:T(8,128)S(1)}, f32[128,128]{1,0:T(8,128)S(1)}, u32[]{:S(2)}, u32[]{:S(2)}) collective-permute-start(f32[128,128]{1,0:T(8,128)S(1)} %add.31), channel_id=1, source_target_pairs={{0,9},{1,8},{2,11},{3,10},{4,13},{5,12},{6,15},{7,14},{8,1},{9,0},... | collective-permute-start | bytes 196616 | tf_op jit(solution)/shard_map/ppermute | solution.py:141
  23.0 4.5 %collective-permute-start.8 = (f32[160,128]{1,0:T(8,128)S(1)}, f32[160,128]{1,0:T(8,128)S(1)}, u32[]{:S(2)}, u32[]{:S(2)}) collective-permute-start(f32[160,128]{1,0:T(8,128)S(1)} %add.36), channel_id=1, source_target_pairs={{0,8},{1,9},{2,10},{3,11},{4,12},{5,13},{6,14},{7,15},{8,0},{9,1},... | collective-permute-start | bytes 245768 | tf_op jit(solution)/shard_map/ppermute | solution.py:141
  25.3 5.1 %collective-permute-start.4 = (f32[128,128]{1,0:T(8,128)S(1)}, f32[128,128]{1,0:T(8,128)S(1)}, u32[]{:S(2)}, u32[]{:S(2)}) collective-permute-start(f32[128,128]{1,0:T(8,128)S(1)} %add.33), channel_id=1, source_target_pairs={{0,17},{1,16},{2,19},{3,18},{4,21},{5,20},{6,23},{7,22},{8,25},{9,... | collective-permute-start | bytes 196616 | tf_op jit(solution)/shard_map/ppermute | solution.py:141
  27.5 8.1 %collective-permute-start.9 = (f32[160,128]{1,0:T(8,128)S(1)}, f32[160,128]{1,0:T(8,128)S(1)}, u32[]{:S(2)}, u32[]{:S(2)}) collective-permute-start(f32[160,128]{1,0:T(8,128)S(1)} %add.38), channel_id=1, source_target_pairs={{0,16},{1,17},{2,18},{3,19},{4,20},{5,21},{6,22},{7,23},{8,24},{9,... | collective-permute-start | bytes 245768 | tf_op jit(solution)/shard_map/ppermute | solution.py:141
  30.4 6.5 %copy-start = (f32[128,512]{1,0:T(8,128)S(1)}, f32[128,512]{1,0:T(8,128)}, u32[]{:S(2)}) copy-start(f32[128,512]{1,0:T(8,128)} %panels_ref.3) | copy-start | bytes 786436
  30.4 7.9 %collective-permute-start.5 = (f32[128,128]{1,0:T(8,128)S(1)}, f32[128,128]{1,0:T(8,128)S(1)}, u32[]{:S(2)}, u32[]{:S(2)}) collective-permute-start(f32[128,128]{1,0:T(8,128)S(1)} %select_add_fusion.1.own_ref), channel_id=1, source_target_pairs={{0,2},{1,3},{2,0},{3,1},{4,7},{5,6},{6,5},{7,4},{8,11},{9,10},{10,... | collective-permute-start | bytes 196616 | tf_op jit(solution)/shard_map/ppermute | solution.py:141
  33.7 4.7 %collective-permute-start.6 = (f32[128,128]{1,0:T(8,128)S(1)}, f32[128,128]{1,0:T(8,128)S(1)}, u32[]{:S(2)}, u32[]{:S(2)}) collective-permute-start(f32[128,128]{1,0:T(8,128)S(1)} %select_add_fusion.1.own_ref), channel_id=1, source_target_pairs={{0,1},{1,0},{2,3},{3,2},{4,5},{5,4},{6,7},{7,6},{8,9},{9,8},{10,11... | collective-permute-start | bytes 196616 | tf_op jit(solution)/shard_map/ppermute | solution.py:141
  35.6 1.3 %copy-start.3 = (s32[2,2]{1,0:T(2,128)S(1)}, s32[2,2]{1,0:T(2,128)}, u32[]{:S(2)}) copy-start(s32[2,2]{1,0:T(2,128)} %targets_ref.3) | copy-start | bytes 52
  35.6 1.3 %collective-permute-start.10 = (f32[64,128]{1,0:T(8,128)S(1)}, f32[64,128]{1,0:T(8,128)S(1)}, u32[]{:S(2)}, u32[]{:S(2)}) collective-permute-start(f32[64,128]{1,0:T(8,128)S(1)} %slice.4), channel_id=1, source_target_pairs={{0,1},{1,0},{2,3},{3,2},{4,5},{5,4},{6,7},{7,6},{8,9},{9,8},{10,11... | collective-permute-start | bytes 98312 | tf_op jit(solution)/shard_map/ppermute | solution.py:141
where the time goes:
time: 40 us; the launch traced here: 39.7 us
  waiting for transfers between devices  16.8 us (42%)
  starting transfers between devices  15.2 us (38%)
  Pallas kernels  5.71 us (14%)
  local copies, waits for them, and re-layouts  1.81 us (5%)
    ppermute x11, waiting for transfers between devices, moved(): return lax.ppermute(value, ('col', 'row'), pairs)  16.8 us
    ppermute x11, starting transfers between devices, moved(): return lax.ppermute(value, ('col', 'row'), pairs)  15.2 us
    pallas_call x4, Pallas kernels, run(): return pl.pallas_call(call, compiler_params=PARAMS, **kwargs)(*args)  5.71 us
    unnamed x10, local copies, waits for them, and re-layouts  1.8 us
  transfers between devices with their start and end apart: 11, of which 8 were waited for; matrix products, arithmetic and copies ran while one was open for 0% of the time, Pallas kernels for 9%

commit v1 on v0

v1 whole, which is shorter than its diff:
```python
import functools

import jax
import jax.numpy as jnp
from jax import lax
from jax.experimental import pallas as pl
from jax.experimental.pallas import tpu as pltpu
from jax.sharding import PartitionSpec as P


BLOCK = 128
HALF = BLOCK // 2
PARAMS = pltpu.CompilerParams(vmem_limit_bytes=8 << 20)
NT = (((1,), (1,)), ((), ()))
SMEM = pl.BlockSpec(memory_space=pltpu.SMEM)
VMEM = pl.BlockSpec(memory_space=pltpu.VMEM)
ANY = pl.BlockSpec(memory_space=pl.ANY)
F32, BF16 = jnp.float32, jnp.bfloat16


def odd(place, bits):
    parity = place & 1
    for k in range(1, bits):
        parity ^= (place >> k) & 1
    return parity


def halves(value):
    high = value.astype(BF16)
    return high, (value - high.astype(F32)).astype(BF16)


def product(left, right):
    dot = functools.partial(lax.dot_general, dimension_numbers=NT, preferred_element_type=F32)
    return dot(left[0], right[0]) + (dot(left[0], right[1]) + dot(left[1], right[0]))


def left_lanes(shape):
    return lax.broadcasted_iota(jnp.int32, shape, 1) < HALF


def split_kernel(rows_ref, high_ref, low_ref):
    high_ref[...], low_ref[...] = halves(rows_ref[...])


def near_kernel(bits, order_ref, pattern_ref, high_ref, low_ref, sibling_ref, out_ref, left_high_ref, left_low_ref, mask_ref):
    row, place = lax.axis_index("row"), lax.axis_index("col")
    supernode, parity = order_ref[place], odd(place, bits)

    def masked(parts, block):
        kept = ([], [])
        for k in range(parts[0].shape[1] // BLOCK):
            present = pattern_ref[supernode, block, k] != 0
            for part, out in zip(parts, kept, strict=True):
                piece = part[:, k * BLOCK : (k + 1) * BLOCK]
                out.append(jnp.where(present, piece, jnp.zeros_like(piece)))
        return [jnp.concatenate(out, axis=1) for out in kept]

    own = masked((high_ref[...], low_ref[...]), row)
    sibling = masked(halves(sibling_ref[...]), row ^ 1)
    diagonal = product(own, own)
    out_ref[0:HALF] = diagonal[0:HALF]
    corner, quarter = diagonal[HALF:], HALF // 2
    turned = pltpu.roll(corner[0:quarter], HALF, axis=1)
    out_ref[HALF : HALF + quarter] = jnp.where(left_lanes(turned.shape), turned, corner[quarter:])
    first = (row & 1) == 0
    shared = product(
        [jnp.where(first, a[0:HALF], b[HALF:]) for a, b in zip(own, sibling, strict=True)],
        [jnp.where(first, b, a) for a, b in zip(own, sibling, strict=True)],
    )
    out_ref[HALF + quarter :] = shared
    plain = (((row >> 1) & 1) ^ parity) == 0
    for kept, mine, theirs in zip((left_high_ref, left_low_ref), own, sibling, strict=True):
        kept[...] = jnp.where(plain, mine, theirs)
    for k in range(mask_ref.shape[1] // BLOCK):
        keep = pattern_ref[supernode, row ^ parity ^ 2, k].astype(F32)
        mask_ref[:, k * BLOCK : (k + 1) * BLOCK] = jnp.full((mask_ref.shape[0], BLOCK), keep)


def far_kernel(mask_ref, high_ref, low_ref, across_ref, out_ref):
    across = halves(across_ref[...] * mask_ref[0:1])
    out_ref[...] = product(across, (high_ref[...], low_ref[...]))


def near_finish_kernel(targets_ref, panels_ref, near_ref, beside_ref, out_ref, which_ref):
    quarter = HALF // 2
    upper = near_ref[0:HALF]
    turned = jnp.concatenate([upper, upper]).T[HALF:]
    corner = near_ref[HALF : HALF + quarter]
    corner = jnp.concatenate([pltpu.roll(corner, HALF, axis=1), corner])
    diagonal = jnp.concatenate([upper, jnp.where(left_lanes(corner.shape), turned, corner)])
    row, per_panel = lax.axis_index("row"), targets_ref.shape[1]
    first = (row & 1) == 0
    mine, theirs = near_ref[HALF + quarter :], beside_ref[...]
    shared = jnp.concatenate([jnp.where(first, mine, theirs), jnp.where(first, theirs, mine)])
    shared = jnp.where(first, shared, shared.T)
    for slot in range(targets_ref.shape[0] * per_panel):
        columns = slice(slot * BLOCK, (slot + 1) * BLOCK)
        j = targets_ref[slot // per_panel, slot % per_panel] ^ row
        near = jnp.where(j == 0, diagonal, jnp.where(j == 1, shared, jnp.zeros_like(shared)))
        out_ref[:, columns] = panels_ref[:, columns] - near
        which_ref[:, columns] = jnp.full((which_ref.shape[0], BLOCK), j)


def far_finish_kernel(bits, which_ref, begun_ref, own_ref, across_ref, beside_ref, out_hbm, staged_ref, sems):
    second = (lax.axis_index("row") >> 1) & 1
    plain, first = (second ^ odd(lax.axis_index("col"), bits)) == 0, second == 0
    turned, straight = jnp.where(plain, own_ref[...], beside_ref[...]).T, across_ref[...]
    two, three = jnp.where(first, turned, straight), jnp.where(first, straight, turned)
    copies = []
    for slot in range(staged_ref.shape[0]):
        columns = slice(slot * BLOCK, (slot + 1) * BLOCK)
        j = which_ref[0:1, columns]
        far = jnp.where(j == 2, two, jnp.where(j == 3, three, 0.0))
        staged_ref[slot] = begun_ref[:, columns] - far
        copies.append(pltpu.make_async_copy(staged_ref.at[slot], out_hbm.at[:, columns], sems.at[slot]))
        copies[-1].start()
    for copy in copies:
        copy.wait()


def moved(value, to):
    columns, rows = lax.axis_size("col"), lax.axis_size("row")
    pairs = []
    for place in range(columns):
        for row in range(rows):
            there, other = to(place, row)
            pairs.append((place * rows + row, there * rows + other))
    return lax.ppermute(value, ("col", "row"), pairs)


def scanned(update, turn):
    place, size = lax.axis_index("col"), lax.axis_size("col")
    inclusive, total, bit = update, update, 1
    while bit < size:
        other = moved(total, lambda p, r, bit=bit: (p ^ bit, r ^ turn))
        inclusive = inclusive + jnp.where((place & bit) != 0, other, 0.0)
        total = total + other
        bit = bit * 2
    return inclusive


def kernel(call, **kwargs):
    def run(*args):
        return pl.pallas_call(call, compiler_params=PARAMS, **kwargs)(*args)

    return run


def body(factor, pattern, order, targets, panels):
    own = factor[0]
    rows, width = own.shape
    bits = (lax.axis_size("col") - 1).bit_length()
    cost = functools.partial(pl.CostEstimate, transcendentals=0)
    flops = 2 * 3 * rows * BLOCK * width
    across = moved(own, lambda p, r: (p, r ^ 2 ^ odd(p, bits)))
    sibling = moved(own, lambda p, r: (p, r ^ 1))
    pair = [jax.ShapeDtypeStruct((rows, width), BF16)] * 2
    high, low = kernel(
        split_kernel,
        out_shape=pair,
        in_specs=[VMEM],
        out_specs=[VMEM] * 2,
        cost_estimate=cost(flops=4 * rows * width, bytes_accessed=8 * rows * width),
    )(own)
    near, high, low, mask = kernel(
        functools.partial(near_kernel, bits),
        out_shape=[jax.ShapeDtypeStruct((BLOCK + HALF // 2, BLOCK), F32), *pair, jax.ShapeDtypeStruct((8, width), F32)],
        in_specs=[SMEM] * 2 + [VMEM] * 3,
        out_specs=[VMEM] * 4,
        cost_estimate=cost(flops=2 * flops, bytes_accessed=12 * rows * width),
    )(order, pattern, high, low, sibling)
    near_sum = scanned(near, 0)
    far = kernel(
        far_kernel,
        out_shape=jax.ShapeDtypeStruct((rows, rows), F32),
        in_specs=[VMEM] * 4,
        out_specs=VMEM,
        cost_estimate=cost(flops=flops, bytes_accessed=8 * rows * width),
    )(mask, high, low, across)
    far_sum = scanned(far, 1)
    shared = moved(near_sum[HALF + HALF // 2 :], lambda p, r: (p, r ^ 1))
    theirs = moved(far_sum, lambda p, r: (p, r ^ 2 ^ odd(p, bits)))
    beside = moved(far_sum, lambda p, r: (p, r ^ 1))
    slots = targets.shape[0] * targets.shape[1]
    writing = cost(flops=0, bytes_accessed=12 * rows * panels.shape[1])
    begun, which = kernel(
        near_finish_kernel,
        out_shape=[jax.ShapeDtypeStruct(panels.shape, F32), jax.ShapeDtypeStruct((8, panels.shape[1]), jnp.int32)],
        in_specs=[SMEM] + [VMEM] * 3,
        out_specs=[VMEM] * 2,
        cost_estimate=writing,
    )(targets, panels, near_sum, shared)
    carried = kernel(
        functools.partial(far_finish_kernel, bits),
        out_shape=jax.ShapeDtypeStruct(panels.shape, F32),
        in_specs=[VMEM] * 5,
        out_specs=ANY,
        scratch_shapes=[pltpu.VMEM((slots, rows, BLOCK), F32), pltpu.SemaphoreType.DMA((slots,))],
        cost_estimate=writing,
    )(which, begun, far_sum, theirs, beside)
    return carried[None]


def solution(mesh):
    placed = (P("col", "row", None), P(), P(), P(), P("row", None))
    return jax.shard_map(
        body, mesh=mesh, in_specs=placed, out_specs=P("col", "row", None), check_vma=False
    )
```

time: 40 us -> 38.1 us (0.953)
  Pallas kernels: 5.71 us -> 3.51 us
  starting transfers between devices: 15.2 us -> 15.7 us
    pallas_call x4 -> x5, Pallas kernels: 5.71 us -> 3.51 us  [run(): return pl.pallas_call(call, compiler_params=PARAMS, **kwargs)(*args)]
    ppermute x11, starting transfers between devices: 15.2 us -> 15.7 us  [moved(): return lax.ppermute(value, ('col', 'row'), pairs)]
  transfers between devices with their start and end apart: 11 -> 11, of which waited for: 8 -> 8; matrix products, arithmetic and copies ran while one was open for 0% -> 0% of each run, Pallas kernels for 9% -> 6%
where the time goes in v1:
time: 38.1 us; the launch traced here: 37.9 us
  waiting for transfers between devices  16.7 us (44%)
  starting transfers between devices  15.7 us (41%)
  Pallas kernels  3.51 us (9%)
  local copies, waits for them, and re-layouts  1.74 us (5%)
    ppermute x11, waiting for transfers between devices, moved(): return lax.ppermute(value, ('col', 'row'), pairs)  16.7 us
    ppermute x11, starting transfers between devices, moved(): return lax.ppermute(value, ('col', 'row'), pairs)  15.7 us
    pallas_call x5, Pallas kernels, run(): return pl.pallas_call(call, compiler_params=PARAMS, **kwargs)(*args)  3.51 us
    unnamed x10, local copies, waits for them, and re-layouts  1.74 us
  transfers between devices with their start and end apart: 11, of which 8 were waited for; matrix products, arithmetic and copies ran while one was open for 0% of the time, Pallas kernels for 6%

profile of v1, /device:TPU:0, one launch (start us, length us, event | category | flops | bytes accessed | tf_op | source)
XLA Modules:
  0.0 37.9 jit_solution(262555920425105302)
XLA Ops:
  0.0 0.5 %collective-permute-start = (f32[128,1024]{1,0:T(8,128)}, f32[128,1024]{1,0:T(8,128)S(1)}, u32[]{:S(2)}, u32[]{:S(2)}) collective-permute-start(f32[128,1024]{1,0:T(8,128)} %bitcast.2), channel_id=1, source_target_pairs={{0,1},{1,0},{2,3},{3,2},{4,5},{5,4},{6,7},{7,6},{8,9},{9,8},{10,11... | collective-permute-start | bytes 1572872 | tf_op jit(solution)/shard_map/ppermute | solution.py:129
  0.5 2.5 %collective-permute-start.5 = (f32[128,1024]{1,0:T(8,128)}, f32[128,1024]{1,0:T(8,128)S(1)}, u32[]{:S(2)}, u32[]{:S(2)}) collective-permute-start(f32[128,1024]{1,0:T(8,128)} %bitcast.3), channel_id=1, source_target_pairs={{0,2},{1,3},{2,0},{3,1},{4,7},{5,6},{6,5},{7,4},{8,11},{9,10},{10,... | collective-permute-start | bytes 1572872 | tf_op jit(solution)/shard_map/ppermute | solution.py:129
  3.0 0.0 copy-start
  3.0 1.1 %copy-done = f32[1,128,1024]{2,1,0:T(8,128)S(1)} copy-done((f32[1,128,1024]{2,1,0:T(8,128)S(1)}, f32[1,128,1024]{2,1,0:T(8,128)}, u32[]{:S(2)}) %copy-start) | copy-done | bytes 524312
  4.0 0.0 copy-start.2
  4.0 0.1 shard_map.55
  4.1 0.0 collective-permute-done.sibling_ref
  4.2 0.0 copy-start.4
  4.2 0.6 %copy-done.2 = s32[8,4,8]{2,1,0:T(4,128)S(1)} copy-done((s32[8,4,8]{2,1,0:T(4,128)S(1)}, s32[8,4,8]{2,1,0:T(4,128)}, u32[]{:S(2)}) %copy-start.2) | copy-done | bytes 1048
  4.8 0.0 copy-done.4
  4.8 1.5 %shard_map.56 = (f32[160,128]{1,0:T(8,128)S(1)}, bf16[128,1024]{1,0:T(8,128)(2,1)S(1)}, bf16[128,1024]{1,0:T(8,128)(2,1)S(1)}, f32[8,1024]{1,0:T(8,128)S(1)}) custom-call(s32[8]{0:T(128)S(1)} %copy-done.4, s32[8,4,8]{2,1,0:T(4,128)S(1)} %copy-done.2, bf16[128,1024]{1,0:T(8,128)(2,1)S(1)} %get-tuple-element.13.high_ref, ...), custom_call_target="tpu_custom_call" | custom-call | flops 201326592 | bytes 1572864 | tf_op jit(solution)/shard_map/pallas_call | solution.py:145
  6.3 9.4 %collective-permute-done.5.across_ref = f32[128,1024]{1,0:T(8,128)S(1)} collective-permute-done((f32[128,1024]{1,0:T(8,128)}, f32[128,1024]{1,0:T(8,128)S(1)}, u32[]{:S(2)}, u32[]{:S(2)}) %collective-permute-start.5) | collective-permute-done | bytes 524320 | tf_op jit(solution)/shard_map/ppermute | solution.py:129
  15.8 0.4 %shard_map.58 = f32[128,128]{1,0:T(8,128)S(1)} custom-call(f32[8,1024]{1,0:T(8,128)S(1)} %get-tuple-element.18.mask_ref, bf16[128,1024]{1,0:T(8,128)(2,1)S(1)} %get-tuple-element.19.high_ref, bf16[128,1024]{1,0:T(8,128)(2,1)S(1)} %get-tuple-element.20.low_ref, f32[128,1024]{1,0:T(8,128)S(1)} %collective-permute-done.5.across_ref), custom_call_target="tpu_custom_call" | custom-call | flops 100663296 | bytes 1048576 | tf_op jit(solution)/shard_map/pallas_call | solution.py:145
  16.2 1.1 %collective-permute-start.6 = (f32[128,128]{1,0:T(8,128)S(1)}, f32[128,128]{1,0:T(8,128)S(1)}, u32[]{:S(2)}, u32[]{:S(2)}) collective-permute-start(f32[128,128]{1,0:T(8,128)S(1)} %shard_map.58), channel_id=1, source_target_pairs={{0,5},{1,4},{2,7},{3,6},{4,1},{5,0},{6,3},{7,2},{8,13},{9,12},{10,... | collective-permute-start | bytes 196616 | tf_op jit(solution)/shard_map/ppermute | solution.py:129
  17.3 0.5 %collective-permute-start.1 = (f32[160,128]{1,0:T(8,128)S(1)}, f32[160,128]{1,0:T(8,128)S(1)}, u32[]{:S(2)}, u32[]{:S(2)}) collective-permute-start(f32[160,128]{1,0:T(8,128)S(1)} %get-tuple-element.15), channel_id=1, source_target_pairs={{0,4},{1,5},{2,6},{3,7},{4,0},{5,1},{6,2},{7,3},{8,12},{9,13},{10,... | collective-permute-start | bytes 245768 | tf_op jit(solution)/shard_map/ppermute | solution.py:129
  17.8 2.7 %collective-permute-done.6 = f32[128,128]{1,0:T(8,128)S(1)} collective-permute-done((f32[128,128]{1,0:T(8,128)S(1)}, f32[128,128]{1,0:T(8,128)S(1)}, u32[]{:S(2)}, u32[]{:S(2)}) %collective-permute-start.6) | collective-permute-done | bytes 65568 | tf_op jit(solution)/shard_map/ppermute | solution.py:129
  20.5 0.8 %collective-permute-start.7 = (f32[128,128]{1,0:T(8,128)S(1)}, f32[128,128]{1,0:T(8,128)S(1)}, u32[]{:S(2)}, u32[]{:S(2)}) collective-permute-start(f32[128,128]{1,0:T(8,128)S(1)} %add.36), channel_id=1, source_target_pairs={{0,9},{1,8},{2,11},{3,10},{4,13},{5,12},{6,15},{7,14},{8,1},{9,0},... | collective-permute-start | bytes 196616 | tf_op jit(solution)/shard_map/ppermute | solution.py:129
  21.3 1.1 %collective-permute-done.1 = f32[160,128]{1,0:T(8,128)S(1)} collective-permute-done((f32[160,128]{1,0:T(8,128)S(1)}, f32[160,128]{1,0:T(8,128)S(1)}, u32[]{:S(2)}, u32[]{:S(2)}) %collective-permute-start.1) | collective-permute-done | bytes 81952 | tf_op jit(solution)/shard_map/ppermute | solution.py:129
  22.4 1.7 %collective-permute-start.2 = (f32[160,128]{1,0:T(8,128)S(1)}, f32[160,128]{1,0:T(8,128)S(1)}, u32[]{:S(2)}, u32[]{:S(2)}) collective-permute-start(f32[160,128]{1,0:T(8,128)S(1)} %add.31), channel_id=1, source_target_pairs={{0,8},{1,9},{2,10},{3,11},{4,12},{5,13},{6,14},{7,15},{8,0},{9,1},... | collective-permute-start | bytes 245768 | tf_op jit(solution)/shard_map/ppermute | solution.py:129
  24.1 0.6 %collective-permute-done.7 = f32[128,128]{1,0:T(8,128)S(1)} collective-permute-done((f32[128,128]{1,0:T(8,128)S(1)}, f32[128,128]{1,0:T(8,128)S(1)}, u32[]{:S(2)}, u32[]{:S(2)}) %collective-permute-start.7) | collective-permute-done | bytes 65568 | tf_op jit(solution)/shard_map/ppermute | solution.py:129
  24.7 2.0 %collective-permute-start.8 = (f32[128,128]{1,0:T(8,128)S(1)}, f32[128,128]{1,0:T(8,128)S(1)}, u32[]{:S(2)}, u32[]{:S(2)}) collective-permute-start(f32[128,128]{1,0:T(8,128)S(1)} %add.38), channel_id=1, source_target_pairs={{0,17},{1,16},{2,19},{3,18},{4,21},{5,20},{6,23},{7,22},{8,25},{9,... | collective-permute-start | bytes 196616 | tf_op jit(solution)/shard_map/ppermute | solution.py:129
  26.7 0.2 collective-permute-done.2
  26.9 2.7 %collective-permute-start.3 = (f32[160,128]{1,0:T(8,128)S(1)}, f32[160,128]{1,0:T(8,128)S(1)}, u32[]{:S(2)}, u32[]{:S(2)}) collective-permute-start(f32[160,128]{1,0:T(8,128)S(1)} %add.33), channel_id=1, source_target_pairs={{0,16},{1,17},{2,18},{3,19},{4,20},{5,21},{6,22},{7,23},{8,24},{9,... | collective-permute-start | bytes 245768 | tf_op jit(solution)/shard_map/ppermute | solution.py:129
  29.7 0.1 collective-permute-done.8
  29.8 0.0 copy-start.1
  29.8 1.8 %collective-permute-start.10 = (f32[128,128]{1,0:T(8,128)S(1)}, f32[128,128]{1,0:T(8,128)S(1)}, u32[]{:S(2)}, u32[]{:S(2)}) collective-permute-start(f32[128,128]{1,0:T(8,128)S(1)} %select_add_fusion.1.own_ref), channel_id=1, source_target_pairs={{0,1},{1,0},{2,3},{3,2},{4,5},{5,4},{6,7},{7,6},{8,9},{9,8},{10,11... | collective-permute-start | bytes 196616 | tf_op jit(solution)/shard_map/ppermute | solution.py:129
  31.6 1.9 %collective-permute-start.9 = (f32[128,128]{1,0:T(8,128)S(1)}, f32[128,128]{1,0:T(8,128)S(1)}, u32[]{:S(2)}, u32[]{:S(2)}) collective-permute-start(f32[128,128]{1,0:T(8,128)S(1)} %select_add_fusion.1.own_ref), channel_id=1, source_target_pairs={{0,2},{1,3},{2,0},{3,1},{4,7},{5,6},{6,5},{7,4},{8,11},{9,10},{10,... | collective-permute-start | bytes 196616 | tf_op jit(solution)/shard_map/ppermute | solution.py:129
  33.5 1.4 %collective-permute-done.3 = f32[160,128]{1,0:T(8,128)S(1)} collective-permute-done((f32[160,128]{1,0:T(8,128)S(1)}, f32[160,128]{1,0:T(8,128)S(1)}, u32[]{:S(2)}, u32[]{:S(2)}) %collective-permute-start.3) | collective-permute-done | bytes 81952 | tf_op jit(solution)/shard_map/ppermute | solution.py:129
  35.0 0.0 copy-start.3
  35.0 0.1 collective-permute-start.4
  35.1 1.2 %collective-permute-done.4.beside_ref = f32[64,128]{1,0:T(8,128)S(1)} collective-permute-done((f32[64,128]{1,0:T(8,128)S(1)}, f32[64,128]{1,0:T(8,128)S(1)}, u32[]{:S(2)}, u32[]{:S(2)}) %collective-permute-start.4) | collective-permute-done | bytes 32800 | tf_op jit(solution)/shard_map/ppermute | solution.py:129
  36.3 0.0 copy-done.1
  36.3 0.0 copy-done.3
  36.3 0.7 %shard_map.57 = (f32[128,512]{1,0:T(8,128)S(1)}, s32[8,512]{1,0:T(8,128)S(1)}) custom-call(s32[2,2]{1,0:T(2,128)S(1)} %copy-done.3, f32[128,512]{1,0:T(8,128)S(1)} %copy-done.1, f32[160,128]{1,0:T(8,128)S(1)} %select_add_fusion.near_ref, f32[64,128]{1,0:T(8,128)S(1)} %collective-permute-done.4.beside_ref), custom_call_target="tpu_custom_call" | custom-call | bytes 786432 | tf_op jit(solution)/shard_map/pallas_call | solution.py:145
  37.0 0.0 collective-permute-done.10.beside_ref
  37.0 0.0 collective-permute-done.9.across_ref
  37.0 0.8 %shard_map.59 = f32[128,512]{1,0:T(8,128)} custom-call(s32[8,512]{1,0:T(8,128)S(1)} %get-tuple-element.16.which_ref, f32[128,512]{1,0:T(8,128)S(1)} %get-tuple-element.17.begun_ref, f32[128,128]{1,0:T(8,128)S(1)} %select_add_fusion.1.own_ref, f32[128,128]{1,0:T(8,128)S(1)} %collective-permute-done.9.across_ref, f32[128,128]{1,0:T(8,128)S(1)} %collective-permute-done.10.beside_ref), custom_call_target="tpu_custom_call" | custom-call | bytes 786432 | tf_op jit(solution)/shard_map/pallas_call | solution.py:145
  (7 shorter events, 0.1 us)
Async XLA Ops:
  0.0 4.1 %collective-permute-start = (f32[128,1024]{1,0:T(8,128)}, f32[128,1024]{1,0:T(8,128)S(1)}, u32[]{:S(2)}, u32[]{:S(2)}) collective-permute-start(f32[128,1024]{1,0:T(8,128)} %bitcast.2), channel_id=1, source_target_pairs={{0,1},{1,0},{2,3},{3,2},{4,5},{5,4},{6,7},{7,6},{8,9},{9,8},{10,11... | collective-permute-start | bytes 1572872 | tf_op jit(solution)/shard_map/ppermute | solution.py:129
  0.5 15.3 %collective-permute-start.5 = (f32[128,1024]{1,0:T(8,128)}, f32[128,1024]{1,0:T(8,128)S(1)}, u32[]{:S(2)}, u32[]{:S(2)}) collective-permute-start(f32[128,1024]{1,0:T(8,128)} %bitcast.3), channel_id=1, source_target_pairs={{0,2},{1,3},{2,0},{3,1},{4,7},{5,6},{6,5},{7,4},{8,11},{9,10},{10,... | collective-permute-start | bytes 1572872 | tf_op jit(solution)/shard_map/ppermute | solution.py:129
  3.0 1.1 %copy-start = (f32[1,128,1024]{2,1,0:T(8,128)S(1)}, f32[1,128,1024]{2,1,0:T(8,128)}, u32[]{:S(2)}) copy-start(f32[1,128,1024]{2,1,0:T(8,128)} %param.5) | copy-start | bytes 1572868
  4.0 0.7 %copy-start.2 = (s32[8,4,8]{2,1,0:T(4,128)S(1)}, s32[8,4,8]{2,1,0:T(4,128)}, u32[]{:S(2)}) copy-start(s32[8,4,8]{2,1,0:T(4,128)} %pattern_ref.1) | copy-start | bytes 3076
  4.2 0.7 %copy-start.4 = (s32[8]{0:T(128)S(1)}, s32[8]{0:T(128)}, u32[]{:S(2)}) copy-start(s32[8]{0:T(128)} %order_ref.1) | copy-start | bytes 100
  16.2 4.3 %collective-permute-start.6 = (f32[128,128]{1,0:T(8,128)S(1)}, f32[128,128]{1,0:T(8,128)S(1)}, u32[]{:S(2)}, u32[]{:S(2)}) collective-permute-start(f32[128,128]{1,0:T(8,128)S(1)} %shard_map.58), channel_id=1, source_target_pairs={{0,5},{1,4},{2,7},{3,6},{4,1},{5,0},{6,3},{7,2},{8,13},{9,12},{10,... | collective-permute-start | bytes 196616 | tf_op jit(solution)/shard_map/ppermute | solution.py:129
  17.3 5.1 %collective-permute-start.1 = (f32[160,128]{1,0:T(8,128)S(1)}, f32[160,128]{1,0:T(8,128)S(1)}, u32[]{:S(2)}, u32[]{:S(2)}) collective-permute-start(f32[160,128]{1,0:T(8,128)S(1)} %get-tuple-element.15), channel_id=1, source_target_pairs={{0,4},{1,5},{2,6},{3,7},{4,0},{5,1},{6,2},{7,3},{8,12},{9,13},{10,... | collective-permute-start | bytes 245768 | tf_op jit(solution)/shard_map/ppermute | solution.py:129
  20.5 4.2 %collective-permute-start.7 = (f32[128,128]{1,0:T(8,128)S(1)}, f32[128,128]{1,0:T(8,128)S(1)}, u32[]{:S(2)}, u32[]{:S(2)}) collective-permute-start(f32[128,128]{1,0:T(8,128)S(1)} %add.36), channel_id=1, source_target_pairs={{0,9},{1,8},{2,11},{3,10},{4,13},{5,12},{6,15},{7,14},{8,1},{9,0},... | collective-permute-start | bytes 196616 | tf_op jit(solution)/shard_map/ppermute | solution.py:129
  22.4 4.5 %collective-permute-start.2 = (f32[160,128]{1,0:T(8,128)S(1)}, f32[160,128]{1,0:T(8,128)S(1)}, u32[]{:S(2)}, u32[]{:S(2)}) collective-permute-start(f32[160,128]{1,0:T(8,128)S(1)} %add.31), channel_id=1, source_target_pairs={{0,8},{1,9},{2,10},{3,11},{4,12},{5,13},{6,14},{7,15},{8,0},{9,1},... | collective-permute-start | bytes 245768 | tf_op jit(solution)/shard_map/ppermute | solution.py:129
  24.7 5.1 %collective-permute-start.8 = (f32[128,128]{1,0:T(8,128)S(1)}, f32[128,128]{1,0:T(8,128)S(1)}, u32[]{:S(2)}, u32[]{:S(2)}) collective-permute-start(f32[128,128]{1,0:T(8,128)S(1)} %add.38), channel_id=1, source_target_pairs={{0,17},{1,16},{2,19},{3,18},{4,21},{5,20},{6,23},{7,22},{8,25},{9,... | collective-permute-start | bytes 196616 | tf_op jit(solution)/shard_map/ppermute | solution.py:129
  26.9 8.1 %collective-permute-start.3 = (f32[160,128]{1,0:T(8,128)S(1)}, f32[160,128]{1,0:T(8,128)S(1)}, u32[]{:S(2)}, u32[]{:S(2)}) collective-permute-start(f32[160,128]{1,0:T(8,128)S(1)} %add.33), channel_id=1, source_target_pairs={{0,16},{1,17},{2,18},{3,19},{4,20},{5,21},{6,22},{7,23},{8,24},{9,... | collective-permute-start | bytes 245768 | tf_op jit(solution)/shard_map/ppermute | solution.py:129
  29.8 6.5 %copy-start.1 = (f32[128,512]{1,0:T(8,128)S(1)}, f32[128,512]{1,0:T(8,128)}, u32[]{:S(2)}) copy-start(f32[128,512]{1,0:T(8,128)} %panels_ref.1) | copy-start | bytes 786436
  29.8 7.2 %collective-permute-start.10 = (f32[128,128]{1,0:T(8,128)S(1)}, f32[128,128]{1,0:T(8,128)S(1)}, u32[]{:S(2)}, u32[]{:S(2)}) collective-permute-start(f32[128,128]{1,0:T(8,128)S(1)} %select_add_fusion.1.own_ref), channel_id=1, source_target_pairs={{0,1},{1,0},{2,3},{3,2},{4,5},{5,4},{6,7},{7,6},{8,9},{9,8},{10,11... | collective-permute-start | bytes 196616 | tf_op jit(solution)/shard_map/ppermute | solution.py:129
  31.6 5.4 %collective-permute-start.9 = (f32[128,128]{1,0:T(8,128)S(1)}, f32[128,128]{1,0:T(8,128)S(1)}, u32[]{:S(2)}, u32[]{:S(2)}) collective-permute-start(f32[128,128]{1,0:T(8,128)S(1)} %select_add_fusion.1.own_ref), channel_id=1, source_target_pairs={{0,2},{1,3},{2,0},{3,1},{4,7},{5,6},{6,5},{7,4},{8,11},{9,10},{10,... | collective-permute-start | bytes 196616 | tf_op jit(solution)/shard_map/ppermute | solution.py:129
  35.0 1.3 %copy-start.3 = (s32[2,2]{1,0:T(2,128)S(1)}, s32[2,2]{1,0:T(2,128)}, u32[]{:S(2)}) copy-start(s32[2,2]{1,0:T(2,128)} %targets_ref.1) | copy-start | bytes 52
  35.0 1.3 %collective-permute-start.4 = (f32[64,128]{1,0:T(8,128)S(1)}, f32[64,128]{1,0:T(8,128)S(1)}, u32[]{:S(2)}, u32[]{:S(2)}) collective-permute-start(f32[64,128]{1,0:T(8,128)S(1)} %slice.4), channel_id=1, source_target_pairs={{0,1},{1,0},{2,3},{3,2},{4,5},{5,4},{6,7},{7,6},{8,9},{9,8},{10,11... | collective-permute-start | bytes 98312 | tf_op jit(solution)/shard_map/ppermute | solution.py:129

commit v2 on v1

--- a/solution.py
+++ b/solution.py
@@ -14,6 +14,7 @@
 NT = (((1,), (1,)), ((), ()))
 SMEM = pl.BlockSpec(memory_space=pltpu.SMEM)
 VMEM = pl.BlockSpec(memory_space=pltpu.VMEM)
+HBM = pl.BlockSpec(memory_space=pltpu.HBM)
 ANY = pl.BlockSpec(memory_space=pl.ANY)
 F32, BF16 = jnp.float32, jnp.bfloat16
 
@@ -39,46 +40,47 @@
     return lax.broadcasted_iota(jnp.int32, shape, 1) < HALF
 
 
-def split_kernel(rows_ref, high_ref, low_ref):
-    high_ref[...], low_ref[...] = halves(rows_ref[...])
-
-
-def near_kernel(bits, order_ref, pattern_ref, high_ref, low_ref, sibling_ref, out_ref, left_high_ref, left_low_ref, mask_ref):
+def split_kernel(bits, order_hbm, pattern_hbm, rows_hbm, high_ref, low_ref, masks_ref, order_ref, cells_ref, rows_ref, sems):
     row, place = lax.axis_index("row"), lax.axis_index("col")
-    supernode, parity = order_ref[place], odd(place, bits)
-
-    def masked(parts, block):
-        kept = ([], [])
-        for k in range(parts[0].shape[1] // BLOCK):
-            present = pattern_ref[supernode, block, k] != 0
-            for part, out in zip(parts, kept, strict=True):
-                piece = part[:, k * BLOCK : (k + 1) * BLOCK]
-                out.append(jnp.where(present, piece, jnp.zeros_like(piece)))
-        return [jnp.concatenate(out, axis=1) for out in kept]
-
-    own = masked((high_ref[...], low_ref[...]), row)
-    sibling = masked(halves(sibling_ref[...]), row ^ 1)
+    rows = pltpu.make_async_copy(rows_hbm, rows_ref, sems.at[0])
+    rows.start()
+    known = pltpu.make_async_copy(order_hbm, order_ref, sems.at[1])
+    known.start()
+    known.wait()
+    cells = pltpu.make_async_copy(pattern_hbm.at[order_ref[place]], cells_ref, sems.at[2])
+    cells.start()
+    cells.wait()
+    for n, block in enumerate((row ^ 1, row ^ odd(place, bits) ^ 2)):
+        for k in range(masks_ref.shape[2] // BLOCK):
+            keep = jnp.full(masks_ref.shape[1:2] + (BLOCK,), cells_ref[block, k].astype(F32))
+            masks_ref[n, :, k * BLOCK : (k + 1) * BLOCK] = keep
+    rows.wait()
+    for k in range(rows_ref.shape[1] // BLOCK):
+        columns = slice(k * BLOCK, (k + 1) * BLOCK)
+        high_ref[:, columns], low_ref[:, columns] = halves(rows_ref[:, columns] * cells_ref[row, k].astype(F32))
+
+
+def near_kernel(bits, masks_ref, high_ref, low_ref, sibling_ref, out_ref, left_high_ref, left_low_ref):
+    row = lax.axis_index("row")
+    own = (high_ref[...], low_ref[...])
+    sibling = halves(sibling_ref[...] * masks_ref[0, 0:1])
     diagonal = product(own, own)
     out_ref[0:HALF] = diagonal[0:HALF]
     corner, quarter = diagonal[HALF:], HALF // 2
     turned = pltpu.roll(corner[0:quarter], HALF, axis=1)
     out_ref[HALF : HALF + quarter] = jnp.where(left_lanes(turned.shape), turned, corner[quarter:])
     first = (row & 1) == 0
-    shared = product(
+    out_ref[HALF + quarter :] = product(
         [jnp.where(first, a[0:HALF], b[HALF:]) for a, b in zip(own, sibling, strict=True)],
         [jnp.where(first, b, a) for a, b in zip(own, sibling, strict=True)],
     )
-    out_ref[HALF + quarter :] = shared
-    plain = (((row >> 1) & 1) ^ parity) == 0
+    plain = (((row >> 1) & 1) ^ odd(lax.axis_index("col"), bits)) == 0
     for kept, mine, theirs in zip((left_high_ref, left_low_ref), own, sibling, strict=True):
         kept[...] = jnp.where(plain, mine, theirs)
-    for k in range(mask_ref.shape[1] // BLOCK):
-        keep = pattern_ref[supernode, row ^ parity ^ 2, k].astype(F32)
-        mask_ref[:, k * BLOCK : (k + 1) * BLOCK] = jnp.full((mask_ref.shape[0], BLOCK), keep)
-
-
-def far_kernel(mask_ref, high_ref, low_ref, across_ref, out_ref):
-    across = halves(across_ref[...] * mask_ref[0:1])
+
+
+def far_kernel(masks_ref, high_ref, low_ref, across_ref, out_ref):
+    across = halves(across_ref[...] * masks_ref[1, 0:1])
     out_ref[...] = product(across, (high_ref[...], low_ref[...]))
 
 
@@ -129,14 +131,25 @@
     return lax.ppermute(value, ("col", "row"), pairs)
 
 
+def steps_of(size):
+    low, steps = 1, []
+    while low < size:
+        steps.append((low, min(4, size // low)))
+        low *= steps[-1][1]
+    return steps
+
+
 def scanned(update, turn):
-    place, size = lax.axis_index("col"), lax.axis_size("col")
-    inclusive, total, bit = update, update, 1
-    while bit < size:
-        other = moved(total, lambda p, r, bit=bit: (p ^ bit, r ^ turn))
-        inclusive = inclusive + jnp.where((place & bit) != 0, other, 0.0)
-        total = total + other
-        bit = bit * 2
+    place = lax.axis_index("col")
+    inclusive, total = update, update
+    for low, count in steps_of(lax.axis_size("col")):
+        others = {
+            flip: moved(total, lambda p, r, flip=flip: (p ^ low * flip, r ^ turn * odd(flip, 2)))
+            for flip in reversed(range(1, count))
+        }
+        digit = (place // low) % count
+        inclusive = inclusive + sum(jnp.where((digit ^ flip) < digit, other, 0.0) for flip, other in others.items())
+        total = total + sum(others.values())
     return inclusive
 
 
@@ -156,20 +169,27 @@
     across = moved(own, lambda p, r: (p, r ^ 2 ^ odd(p, bits)))
     sibling = moved(own, lambda p, r: (p, r ^ 1))
     pair = [jax.ShapeDtypeStruct((rows, width), BF16)] * 2
-    high, low = kernel(
-        split_kernel,
-        out_shape=pair,
-        in_specs=[VMEM],
-        out_specs=[VMEM] * 2,
+    held = functools.partial(pltpu.with_memory_space_constraint, memory_space=pltpu.HBM)
+    high, low, masks = kernel(
+        functools.partial(split_kernel, bits),
+        out_shape=[*pair, jax.ShapeDtypeStruct((2, 8, width), F32)],
+        in_specs=[HBM] * 3,
+        out_specs=[VMEM] * 3,
+        scratch_shapes=[
+            pltpu.SMEM(order.shape, jnp.int32),
+            pltpu.SMEM(pattern.shape[1:], jnp.int32),
+            pltpu.VMEM((rows, width), F32),
+            pltpu.SemaphoreType.DMA((3,)),
+        ],
         cost_estimate=cost(flops=4 * rows * width, bytes_accessed=8 * rows * width),
-    )(own)
-    near, high, low, mask = kernel(
+    )(held(order), held(pattern), held(own))
+    near, high, low = kernel(
         functools.partial(near_kernel, bits),
-        out_shape=[jax.ShapeDtypeStruct((BLOCK + HALF // 2, BLOCK), F32), *pair, jax.ShapeDtypeStruct((8, width), F32)],
-        in_specs=[SMEM] * 2 + [VMEM] * 3,
-        out_specs=[VMEM] * 4,
+        out_shape=[jax.ShapeDtypeStruct((BLOCK + HALF // 2, BLOCK), F32), *pair],
+        in_specs=[VMEM] * 4,
+        out_specs=[VMEM] * 3,
         cost_estimate=cost(flops=2 * flops, bytes_accessed=12 * rows * width),
-    )(order, pattern, high, low, sibling)
+    )(masks, high, low, sibling)
     near_sum = scanned(near, 0)
     far = kernel(
         far_kernel,
@@ -177,7 +197,7 @@
         in_specs=[VMEM] * 4,
         out_specs=VMEM,
         cost_estimate=cost(flops=flops, bytes_accessed=8 * rows * width),
-    )(mask, high, low, across)
+    )(masks, high, low, across)
     far_sum = scanned(far, 1)
     shared = moved(near_sum[HALF + HALF // 2 :], lambda p, r: (p, r ^ 1))
     theirs = moved(far_sum, lambda p, r: (p, r ^ 2 ^ odd(p, bits)))

time: 38.1 us -> 38 us (level)
  local copies, waits for them, and re-layouts: 1.74 us -> 0.02 us
  Pallas kernels: 3.51 us -> 4.28 us
  waiting for transfers between devices: 16.7 us -> 17.3 us
    unnamed x10 -> x4, local copies, waits for them, and re-layouts: 1.74 us -> 0.01 us
    pallas_call x5, Pallas kernels: 3.51 us -> 4.28 us  [run(): return pl.pallas_call(call, compiler_params=PARAMS, **kwargs)(*args)]
    ppermute x11 -> x13, waiting for transfers between devices: 16.7 us -> 17.3 us  [moved(): return lax.ppermute(value, ('col', 'row'), pairs)]
    ppermute x11 -> x13, starting transfers between devices: 15.7 us -> 16 us  [moved(): return lax.ppermute(value, ('col', 'row'), pairs)]
  transfers between devices with their start and end apart: 11 -> 13, of which waited for: 8 -> 5; matrix products, arithmetic and copies ran while one was open for 0% -> 0% of each run, Pallas kernels for 6% -> 8%
where the time goes in v2:
time: 38 us; the launch traced here: 37.8 us
  waiting for transfers between devices  17.3 us (46%)
  starting transfers between devices  16 us (42%)
  Pallas kernels  4.28 us (11%)
    ppermute x13, waiting for transfers between devices, moved(): return lax.ppermute(value, ('col', 'row'), pairs)  17.3 us
    ppermute x13, starting transfers between devices, moved(): return lax.ppermute(value, ('col', 'row'), pairs)  16 us
    pallas_call x5, Pallas kernels, run(): return pl.pallas_call(call, compiler_params=PARAMS, **kwargs)(*args)  4.28 us
  transfers between devices with their start and end apart: 13, of which 5 were waited for; matrix products, arithmetic and copies ran while one was open for 0% of the time, Pallas kernels for 8%

profile of v2, /device:TPU:0, one launch (start us, length us, event | category | flops | bytes accessed | tf_op | source)
XLA Modules:
  0.0 37.8 jit_solution(11028530139230152062)
XLA Ops:
  0.0 0.5 %collective-permute-start = (f32[128,1024]{1,0:T(8,128)}, f32[128,1024]{1,0:T(8,128)S(1)}, u32[]{:S(2)}, u32[]{:S(2)}) collective-permute-start(f32[128,1024]{1,0:T(8,128)} %bitcast.2), channel_id=1, source_target_pairs={{0,1},{1,0},{2,3},{3,2},{4,5},{5,4},{6,7},{7,6},{8,9},{9,8},{10,11... | collective-permute-start | bytes 1572872 | tf_op jit(solution)/shard_map/ppermute | solution.py:131
  0.5 2.5 %collective-permute-start.6 = (f32[128,1024]{1,0:T(8,128)}, f32[128,1024]{1,0:T(8,128)S(1)}, u32[]{:S(2)}, u32[]{:S(2)}) collective-permute-start(f32[128,1024]{1,0:T(8,128)} %bitcast.3), channel_id=1, source_target_pairs={{0,2},{1,3},{2,0},{3,1},{4,7},{5,6},{6,5},{7,4},{8,11},{9,10},{10,... | collective-permute-start | bytes 1572872 | tf_op jit(solution)/shard_map/ppermute | solution.py:131
  3.0 1.7 %shard_map.55 = (bf16[128,1024]{1,0:T(8,128)(2,1)S(1)}, bf16[128,1024]{1,0:T(8,128)(2,1)S(1)}, f32[2,8,1024]{2,1,0:T(8,128)S(1)}) custom-call(s32[8]{0:T(128)} %order_hbm.1, s32[8,4,8]{2,1,0:T(4,128)} %pattern_hbm.1, f32[128,1024]{1,0:T(8,128)} %bitcast.4), custom_call_target="tpu_custom_call" | custom-call | flops 524288 | bytes 1048576 | tf_op jit(solution)/shard_map/pallas_call | solution.py:158
  4.7 0.0 collective-permute-done.sibling_ref
  4.7 0.7 %shard_map.56 = (f32[160,128]{1,0:T(8,128)S(1)}, bf16[128,1024]{1,0:T(8,128)(2,1)S(1)}, bf16[128,1024]{1,0:T(8,128)(2,1)S(1)}) custom-call(f32[2,8,1024]{2,1,0:T(8,128)S(1)} %get-tuple-element.13.masks_ref, bf16[128,1024]{1,0:T(8,128)(2,1)S(1)} %get-tuple-element.14.high_ref, bf16[128,1024]{1,0:T(8,128)(2,1)S(1)} %get-tuple-element.15.low_ref, ...), custom_call_target="tpu_custom_call" | custom-call | flops 201326592 | bytes 1572864 | tf_op jit(solution)/shard_map/pallas_call | solution.py:158
  5.4 10.4 %collective-permute-done.6.across_ref = f32[128,1024]{1,0:T(8,128)S(1)} collective-permute-done((f32[128,1024]{1,0:T(8,128)}, f32[128,1024]{1,0:T(8,128)S(1)}, u32[]{:S(2)}, u32[]{:S(2)}) %collective-permute-start.6) | collective-permute-done | bytes 524320 | tf_op jit(solution)/shard_map/ppermute | solution.py:131
  15.8 0.4 %shard_map.58 = f32[128,128]{1,0:T(8,128)S(1)} custom-call(f32[2,8,1024]{2,1,0:T(8,128)S(1)} %get-tuple-element.13.masks_ref, bf16[128,1024]{1,0:T(8,128)(2,1)S(1)} %get-tuple-element.19.high_ref, bf16[128,1024]{1,0:T(8,128)(2,1)S(1)} %get-tuple-element.20.low_ref, f32[128,1024]{1,0:T(8,128)S(1)} %collective-permute-done.6.across_ref), custom_call_target="tpu_custom_call" | custom-call | flops 100663296 | bytes 1048576 | tf_op jit(solution)/shard_map/pallas_call | solution.py:158
  16.2 2.8 %collective-permute-start.7 = (f32[128,128]{1,0:T(8,128)S(1)}, f32[128,128]{1,0:T(8,128)S(1)}, u32[]{:S(2)}, u32[]{:S(2)}) collective-permute-start(f32[128,128]{1,0:T(8,128)S(1)} %shard_map.58), channel_id=1, source_target_pairs={{0,12},{1,13},{2,14},{3,15},{4,8},{5,9},{6,10},{7,11},{8,4},{9,5},... | collective-permute-start | bytes 196616 | tf_op jit(solution)/shard_map/ppermute | solution.py:131
  19.0 0.0 collective-permute-start.8
  19.0 0.4 %collective-permute-start.9 = (f32[128,128]{1,0:T(8,128)S(1)}, f32[128,128]{1,0:T(8,128)S(1)}, u32[]{:S(2)}, u32[]{:S(2)}) collective-permute-start(f32[128,128]{1,0:T(8,128)S(1)} %shard_map.58), channel_id=1, source_target_pairs={{0,5},{1,4},{2,7},{3,6},{4,1},{5,0},{6,3},{7,2},{8,13},{9,12},{10,... | collective-permute-start | bytes 196616 | tf_op jit(solution)/shard_map/ppermute | solution.py:131
  19.4 2.8 %collective-permute-start.1 = (f32[160,128]{1,0:T(8,128)S(1)}, f32[160,128]{1,0:T(8,128)S(1)}, u32[]{:S(2)}, u32[]{:S(2)}) collective-permute-start(f32[160,128]{1,0:T(8,128)S(1)} %get-tuple-element.16), channel_id=1, source_target_pairs={{0,12},{1,13},{2,14},{3,15},{4,8},{5,9},{6,10},{7,11},{8,4},{9,5},... | collective-permute-start | bytes 245768 | tf_op jit(solution)/shard_map/ppermute | solution.py:131
  22.2 0.0 collective-permute-start.2
  22.2 0.0 collective-permute-done.7
  22.2 0.7 %collective-permute-start.3 = (f32[160,128]{1,0:T(8,128)S(1)}, f32[160,128]{1,0:T(8,128)S(1)}, u32[]{:S(2)}, u32[]{:S(2)}) collective-permute-start(f32[160,128]{1,0:T(8,128)S(1)} %get-tuple-element.16), channel_id=1, source_target_pairs={{0,4},{1,5},{2,6},{3,7},{4,0},{5,1},{6,2},{7,3},{8,12},{9,13},{10,... | collective-permute-start | bytes 245768 | tf_op jit(solution)/shard_map/ppermute | solution.py:131
  22.9 0.0 collective-permute-done.8
  22.9 2.0 %collective-permute-done.9 = f32[128,128]{1,0:T(8,128)S(1)} collective-permute-done((f32[128,128]{1,0:T(8,128)S(1)}, f32[128,128]{1,0:T(8,128)S(1)}, u32[]{:S(2)}, u32[]{:S(2)}) %collective-permute-start.9) | collective-permute-done | bytes 65568 | tf_op jit(solution)/shard_map/ppermute | solution.py:131
  25.0 2.5 %collective-permute-start.10 = (f32[128,128]{1,0:T(8,128)S(1)}, f32[128,128]{1,0:T(8,128)S(1)}, u32[]{:S(2)}, u32[]{:S(2)}) collective-permute-start(f32[128,128]{1,0:T(8,128)S(1)} %add_add_fusion.1), channel_id=1, source_target_pairs={{0,17},{1,16},{2,19},{3,18},{4,21},{5,20},{6,23},{7,22},{8,25},{9,... | collective-permute-start | bytes 196616 | tf_op jit(solution)/shard_map/ppermute | solution.py:131
  27.5 0.0 collective-permute-done.1
  27.5 0.0 collective-permute-done.2
  27.5 0.0 collective-permute-done.3
  27.6 2.2 %collective-permute-start.4 = (f32[160,128]{1,0:T(8,128)S(1)}, f32[160,128]{1,0:T(8,128)S(1)}, u32[]{:S(2)}, u32[]{:S(2)}) collective-permute-start(f32[160,128]{1,0:T(8,128)S(1)} %add_add_fusion), channel_id=1, source_target_pairs={{0,16},{1,17},{2,18},{3,19},{4,20},{5,21},{6,22},{7,23},{8,24},{9,... | collective-permute-start | bytes 245768 | tf_op jit(solution)/shard_map/ppermute | solution.py:131
  29.8 0.9 %collective-permute-done.10 = f32[128,128]{1,0:T(8,128)S(1)} collective-permute-done((f32[128,128]{1,0:T(8,128)S(1)}, f32[128,128]{1,0:T(8,128)S(1)}, u32[]{:S(2)}, u32[]{:S(2)}) %collective-permute-start.10) | collective-permute-done | bytes 65568 | tf_op jit(solution)/shard_map/ppermute | solution.py:131
  30.8 0.0 copy-start
  30.8 1.5 %collective-permute-start.11 = (f32[128,128]{1,0:T(8,128)S(1)}, f32[128,128]{1,0:T(8,128)S(1)}, u32[]{:S(2)}, u32[]{:S(2)}) collective-permute-start(f32[128,128]{1,0:T(8,128)S(1)} %select_add_fusion.1.own_ref), channel_id=1, source_target_pairs={{0,2},{1,3},{2,0},{3,1},{4,7},{5,6},{6,5},{7,4},{8,11},{9,10},{10,... | collective-permute-start | bytes 196616 | tf_op jit(solution)/shard_map/ppermute | solution.py:131
  32.2 0.0 collective-permute-start.12
  32.2 2.7 %collective-permute-done.4 = f32[160,128]{1,0:T(8,128)S(1)} collective-permute-done((f32[160,128]{1,0:T(8,128)S(1)}, f32[160,128]{1,0:T(8,128)S(1)}, u32[]{:S(2)}, u32[]{:S(2)}) %collective-permute-start.4) | collective-permute-done | bytes 81952 | tf_op jit(solution)/shard_map/ppermute | solution.py:131
  35.0 0.0 copy-start.1
  35.0 0.1 collective-permute-start.5
  35.1 1.2 %collective-permute-done.5.beside_ref = f32[64,128]{1,0:T(8,128)S(1)} collective-permute-done((f32[64,128]{1,0:T(8,128)S(1)}, f32[64,128]{1,0:T(8,128)S(1)}, u32[]{:S(2)}, u32[]{:S(2)}) %collective-permute-start.5) | collective-permute-done | bytes 32800 | tf_op jit(solution)/shard_map/ppermute | solution.py:131
  36.3 0.0 copy-done
  36.3 0.0 copy-done.1
  36.3 0.7 %shard_map.57 = (f32[128,512]{1,0:T(8,128)S(1)}, s32[8,512]{1,0:T(8,128)S(1)}) custom-call(s32[2,2]{1,0:T(2,128)S(1)} %copy-done.1, f32[128,512]{1,0:T(8,128)S(1)} %copy-done, f32[160,128]{1,0:T(8,128)S(1)} %select_add_fusion.near_ref, f32[64,128]{1,0:T(8,128)S(1)} %collective-permute-done.5.beside_ref), custom_call_target="tpu_custom_call" | custom-call | bytes 786432 | tf_op jit(solution)/shard_map/pallas_call | solution.py:158
  37.0 0.0 collective-permute-done.11.across_ref
  37.0 0.0 collective-permute-done.12.beside_ref
  37.0 0.8 %shard_map.59 = f32[128,512]{1,0:T(8,128)} custom-call(s32[8,512]{1,0:T(8,128)S(1)} %get-tuple-element.17.which_ref, f32[128,512]{1,0:T(8,128)S(1)} %get-tuple-element.18.begun_ref, f32[128,128]{1,0:T(8,128)S(1)} %select_add_fusion.1.own_ref, f32[128,128]{1,0:T(8,128)S(1)} %collective-permute-done.11.across_ref, ...), custom_call_target="tpu_custom_call" | custom-call | bytes 786432 | tf_op jit(solution)/shard_map/pallas_call | solution.py:158
  (5 shorter events, 0.1 us)
Async XLA Ops:
  0.0 4.7 %collective-permute-start = (f32[128,1024]{1,0:T(8,128)}, f32[128,1024]{1,0:T(8,128)S(1)}, u32[]{:S(2)}, u32[]{:S(2)}) collective-permute-start(f32[128,1024]{1,0:T(8,128)} %bitcast.2), channel_id=1, source_target_pairs={{0,1},{1,0},{2,3},{3,2},{4,5},{5,4},{6,7},{7,6},{8,9},{9,8},{10,11... | collective-permute-start | bytes 1572872 | tf_op jit(solution)/shard_map/ppermute | solution.py:131
  0.5 15.3 %collective-permute-start.6 = (f32[128,1024]{1,0:T(8,128)}, f32[128,1024]{1,0:T(8,128)S(1)}, u32[]{:S(2)}, u32[]{:S(2)}) collective-permute-start(f32[128,1024]{1,0:T(8,128)} %bitcast.3), channel_id=1, source_target_pairs={{0,2},{1,3},{2,0},{3,1},{4,7},{5,6},{6,5},{7,4},{8,11},{9,10},{10,... | collective-permute-start | bytes 1572872 | tf_op jit(solution)/shard_map/ppermute | solution.py:131
  16.2 6.1 %collective-permute-start.7 = (f32[128,128]{1,0:T(8,128)S(1)}, f32[128,128]{1,0:T(8,128)S(1)}, u32[]{:S(2)}, u32[]{:S(2)}) collective-permute-start(f32[128,128]{1,0:T(8,128)S(1)} %shard_map.58), channel_id=1, source_target_pairs={{0,12},{1,13},{2,14},{3,15},{4,8},{5,9},{6,10},{7,11},{8,4},{9,5},... | collective-permute-start | bytes 196616 | tf_op jit(solution)/shard_map/ppermute | solution.py:131
  19.0 3.9 %collective-permute-start.8 = (f32[128,128]{1,0:T(8,128)S(1)}, f32[128,128]{1,0:T(8,128)S(1)}, u32[]{:S(2)}, u32[]{:S(2)}) collective-permute-start(f32[128,128]{1,0:T(8,128)S(1)} %shard_map.58), channel_id=1, source_target_pairs={{0,9},{1,8},{2,11},{3,10},{4,13},{5,12},{6,15},{7,14},{8,1},{9,0},... | collective-permute-start | bytes 196616 | tf_op jit(solution)/shard_map/ppermute | solution.py:131
  19.0 6.0 %collective-permute-start.9 = (f32[128,128]{1,0:T(8,128)S(1)}, f32[128,128]{1,0:T(8,128)S(1)}, u32[]{:S(2)}, u32[]{:S(2)}) collective-permute-start(f32[128,128]{1,0:T(8,128)S(1)} %shard_map.58), channel_id=1, source_target_pairs={{0,5},{1,4},{2,7},{3,6},{4,1},{5,0},{6,3},{7,2},{8,13},{9,12},{10,... | collective-permute-start | bytes 196616 | tf_op jit(solution)/shard_map/ppermute | solution.py:131
  19.4 8.1 %collective-permute-start.1 = (f32[160,128]{1,0:T(8,128)S(1)}, f32[160,128]{1,0:T(8,128)S(1)}, u32[]{:S(2)}, u32[]{:S(2)}) collective-permute-start(f32[160,128]{1,0:T(8,128)S(1)} %get-tuple-element.16), channel_id=1, source_target_pairs={{0,12},{1,13},{2,14},{3,15},{4,8},{5,9},{6,10},{7,11},{8,4},{9,5},... | collective-permute-start | bytes 245768 | tf_op jit(solution)/shard_map/ppermute | solution.py:131
  22.2 5.3 %collective-permute-start.2 = (f32[160,128]{1,0:T(8,128)S(1)}, f32[160,128]{1,0:T(8,128)S(1)}, u32[]{:S(2)}, u32[]{:S(2)}) collective-permute-start(f32[160,128]{1,0:T(8,128)S(1)} %get-tuple-element.16), channel_id=1, source_target_pairs={{0,8},{1,9},{2,10},{3,11},{4,12},{5,13},{6,14},{7,15},{8,0},{9,1},... | collective-permute-start | bytes 245768 | tf_op jit(solution)/shard_map/ppermute | solution.py:131
  22.2 5.3 %collective-permute-start.3 = (f32[160,128]{1,0:T(8,128)S(1)}, f32[160,128]{1,0:T(8,128)S(1)}, u32[]{:S(2)}, u32[]{:S(2)}) collective-permute-start(f32[160,128]{1,0:T(8,128)S(1)} %get-tuple-element.16), channel_id=1, source_target_pairs={{0,4},{1,5},{2,6},{3,7},{4,0},{5,1},{6,2},{7,3},{8,12},{9,13},{10,... | collective-permute-start | bytes 245768 | tf_op jit(solution)/shard_map/ppermute | solution.py:131
  25.0 5.7 %collective-permute-start.10 = (f32[128,128]{1,0:T(8,128)S(1)}, f32[128,128]{1,0:T(8,128)S(1)}, u32[]{:S(2)}, u32[]{:S(2)}) collective-permute-start(f32[128,128]{1,0:T(8,128)S(1)} %add_add_fusion.1), channel_id=1, source_target_pairs={{0,17},{1,16},{2,19},{3,18},{4,21},{5,20},{6,23},{7,22},{8,25},{9,... | collective-permute-start | bytes 196616 | tf_op jit(solution)/shard_map/ppermute | solution.py:131
  27.6 7.4 %collective-permute-start.4 = (f32[160,128]{1,0:T(8,128)S(1)}, f32[160,128]{1,0:T(8,128)S(1)}, u32[]{:S(2)}, u32[]{:S(2)}) collective-permute-start(f32[160,128]{1,0:T(8,128)S(1)} %add_add_fusion), channel_id=1, source_target_pairs={{0,16},{1,17},{2,18},{3,19},{4,20},{5,21},{6,22},{7,23},{8,24},{9,... | collective-permute-start | bytes 245768 | tf_op jit(solution)/shard_map/ppermute | solution.py:131
  30.8 5.5 %copy-start = (f32[128,512]{1,0:T(8,128)S(1)}, f32[128,512]{1,0:T(8,128)}, u32[]{:S(2)}) copy-start(f32[128,512]{1,0:T(8,128)} %panels_ref.1) | copy-start | bytes 786436
  30.8 6.2 %collective-permute-start.11 = (f32[128,128]{1,0:T(8,128)S(1)}, f32[128,128]{1,0:T(8,128)S(1)}, u32[]{:S(2)}, u32[]{:S(2)}) collective-permute-start(f32[128,128]{1,0:T(8,128)S(1)} %select_add_fusion.1.own_ref), channel_id=1, source_target_pairs={{0,2},{1,3},{2,0},{3,1},{4,7},{5,6},{6,5},{7,4},{8,11},{9,10},{10,... | collective-permute-start | bytes 196616 | tf_op jit(solution)/shard_map/ppermute | solution.py:131
  32.2 4.7 %collective-permute-start.12 = (f32[128,128]{1,0:T(8,128)S(1)}, f32[128,128]{1,0:T(8,128)S(1)}, u32[]{:S(2)}, u32[]{:S(2)}) collective-permute-start(f32[128,128]{1,0:T(8,128)S(1)} %select_add_fusion.1.own_ref), channel_id=1, source_target_pairs={{0,1},{1,0},{2,3},{3,2},{4,5},{5,4},{6,7},{7,6},{8,9},{9,8},{10,11... | collective-permute-start | bytes 196616 | tf_op jit(solution)/shard_map/ppermute | solution.py:131
  35.0 1.3 %copy-start.1 = (s32[2,2]{1,0:T(2,128)S(1)}, s32[2,2]{1,0:T(2,128)}, u32[]{:S(2)}) copy-start(s32[2,2]{1,0:T(2,128)} %targets_ref.1) | copy-start | bytes 52
  35.0 1.3 %collective-permute-start.5 = (f32[64,128]{1,0:T(8,128)S(1)}, f32[64,128]{1,0:T(8,128)S(1)}, u32[]{:S(2)}, u32[]{:S(2)}) collective-permute-start(f32[64,128]{1,0:T(8,128)S(1)} %slice.4), channel_id=1, source_target_pairs={{0,1},{1,0},{2,3},{3,2},{4,5},{5,4},{6,7},{7,6},{8,9},{9,8},{10,11... | collective-permute-start | bytes 98312 | tf_op jit(solution)/shard_map/ppermute | solution.py:131
